TPU v7x, 32 devices: a whole 2x2x4 slice. The times are simulated.
32 devices in a mesh: blk: 8 (over y, x, core), feat: 4 (over z).
Axes of the slice: x: 2, y: 2, z: 4, core: 2. Of those that a mesh axis runs over, the one named last changes fastest.
Arguments:
- features: bfloat16 [24576, 512], P('blk', 'feat'), may hold values from -6 to 6
- tile_values: bfloat16 [1024, 128, 128], P('blk'), may hold values from -0.375 to 0.375
- tile_rows: int32 [1024], P('blk'), may hold values from 0 to 23, as said below
- tile_cols: int32 [1024], P('blk'), may hold values from 0 to 23, as said below
- tile_counts: int32 [64], P('blk'), may hold values from 1 to 16, as said below
- weight: bfloat16 [512, 512], replicated, may hold values from -0.25 to 0.25
- bias: float32 [512], P('feat'), may hold values from -3 to 3
Outputs:
- hidden: bfloat16 [24576, 512], P('blk', 'feat')
Inputs may be any that keep to these rules, and one draw needn't show every extreme that they name: `tile_rows`: the live slots of one node block and offset name distinct pairs of row and column tiles. `tile_cols`: paired with tile_rows slot by slot. `tile_counts`: some block and offset has all 16 slots live in every draw.
All inputs are finite; a program needn't handle non-finite values.
Results may differ from a plain program's by a relative error of at most 0.0049.
Values may be sent and summed in bfloat16 or wider, within the bound.
No kernel may reach another device: no remote copies, remote signals or barrier semaphores. Data moves between devices by JAX's collectives and lax.ppermute only.
A program may use at most 64 MiB of HBM per device.

v0:
```python
import jax
import jax.numpy as jnp
from jax import lax
from jax.sharding import PartitionSpec as P


def shifted(shard, axis, by):
    count = lax.axis_size(axis)
    return lax.ppermute(shard, axis, [(i, (i + by) % count) for i in range(count)])


def pick_tiles(current, wanted, row_tiles, tile_size):
    source = current.reshape(row_tiles, tile_size, current.shape[-1])
    return jnp.take(source, wanted, axis=0)


def add_tiles(totals, picked, offset, values_all, row_ids, tile_counts):
    row_tiles = totals.shape[0]
    slot_count = row_ids.shape[1]
    products = jnp.einsum(
        "ktj,kjf->ktf", values_all[offset], picked, preferred_element_type=jnp.float32
    )
    active = jnp.arange(slot_count) < tile_counts[offset]
    one_hot = (
        (row_ids[offset][None, :] == jnp.arange(row_tiles)[:, None]) & active[None, :]
    ).astype(jnp.float32)
    return totals + jnp.einsum("rk,ktf->rtf", one_hot, products, precision=lax.Precision.HIGHEST)


def body(features, tile_values, tile_rows, tile_cols, tile_counts, weight, bias):
    row_count, col_width = features.shape
    tile_size = tile_values.shape[-1]
    row_tiles = row_count // tile_size
    steps_all = tile_counts.shape[0]
    slot_count = tile_rows.shape[0] // steps_all
    values_all = tile_values.reshape(steps_all, slot_count, tile_size, tile_size)
    row_ids = tile_rows.reshape(steps_all, slot_count)
    col_ids = tile_cols.reshape(steps_all, slot_count)
    totals = jnp.zeros((row_tiles, tile_size, col_width), jnp.float32)
    own_picked = pick_tiles(features, col_ids[0], row_tiles, tile_size)
    totals = add_tiles(totals, own_picked, 0, values_all, row_ids, tile_counts)
    current = features
    for offset in range(1, steps_all):
        current = shifted(current, "blk", 1)
        picked = pick_tiles(current, col_ids[offset], row_tiles, tile_size)
        totals = add_tiles(totals, picked, offset, values_all, row_ids, tile_counts)
    aggregate = totals.reshape(row_count, col_width).astype(jnp.bfloat16)
    out_width = bias.shape[0]
    member = lax.axis_index("feat")
    own_cols = lax.dynamic_slice_in_dim(weight, member * out_width, out_width, 1)
    mixed = jnp.dot(
        lax.all_gather(aggregate, "feat", axis=1, tiled=True),
        own_cols,
        preferred_element_type=jnp.float32,
    )
    return jnp.maximum(mixed + bias[None, :], 0.0).astype(jnp.bfloat16)


def solution(mesh):
    in_specs = (
        P("blk", "feat"),
        P("blk", None, None),
        P("blk"),
        P("blk"),
        P("blk"),
        P(),
        P("feat"),
    )
    out_specs = P("blk", "feat")
    return jax.shard_map(body, mesh=mesh, in_specs=in_specs, out_specs=out_specs, check_vma=False)
```

profile of v0, /device:TPU:0, one launch (start us, length us, event | category | flops | bytes accessed | tf_op | source)
XLA Modules:
  0.0 183.8 jit_solution(13651544771678281297)
XLA Ops:
  6.5 0.0 all-gather.2.cloned.1.call-start
  6.5 0.5 collective-permute-start
  7.0 1.0 compare_and_fusion
  8.0 1.6 fusion.107
  9.7 1.8 gather_fusion
  11.5 0.6 iota_compare_fusion.9
  12.1 0.7 iota_compare_fusion.10
  12.8 0.7 iota_compare_fusion.11
  13.5 0.7 iota_compare_fusion.12
  14.2 0.6 iota_compare_fusion.13
  14.7 0.6 iota_compare_fusion.14
  15.4 4.4 %collective-permute-done = bf16[3072,128]{1,0:T(8,128)(2,1)S(1)} collective-permute-done((bf16[3072,128]{1,0:T(8,128)(2,1)}, bf16[3072,128]{1,0:T(8,128)(2,1)S(1)}, u32[]{:S(2)}, u32[]{:S(2)}) %collective-permute-start) | collective-permute-done | bytes 786464 | tf_op jit(solution)/shard_map/ppermute | solution.py:9
  19.8 0.0 collective-permute-start.1
  19.8 0.5 iota_compare_fusion.15
  20.4 1.7 fusion.31
  22.1 10.1 %collective-permute-done.1 = bf16[3072,128]{1,0:T(8,128)(2,1)} collective-permute-done((bf16[3072,128]{1,0:T(8,128)(2,1)S(1)}, bf16[3072,128]{1,0:T(8,128)(2,1)}, u32[]{:S(2)}, u32[]{:S(2)}) %collective-permute-start.1) | collective-permute-done | bytes 786464 | tf_op jit(solution)/shard_map/ppermute | solution.py:9
  32.2 0.0 collective-permute-start.2
  32.2 0.0 copy-done.1
  32.2 0.6 iota_compare_fusion.8
  32.8 0.5 copy.9
  33.4 0.1 fusion.108
  33.5 0.9 fusion.15
  34.4 1.8 gather_fusion.1
  36.2 8.7 %collective-permute-done.2 = bf16[3072,128]{1,0:T(8,128)(2,1)} collective-permute-done((bf16[3072,128]{1,0:T(8,128)(2,1)}, bf16[3072,128]{1,0:T(8,128)(2,1)}, u32[]{:S(2)}, u32[]{:S(2)}) %collective-permute-start.2) | collective-permute-done | bytes 786464 | tf_op jit(solution)/shard_map/ppermute | solution.py:9
  44.8 0.0 collective-permute-start.3
  44.8 2.7 %fusion.29 = f32[16,128,128]{2,1,0:T(8,128)} fusion(bf16[16,128,128]{2,1,0:T(8,128)(2,1)S(1)} %gather_fusion.1, bf16[128,128,128]{2,1,0:T(8,128)(2,1)} %param.10, pred[16]{0:T(512)(128)(4,1)S(1)} %get-tuple-element.46), kind=kOutput, calls=%fused_computation.39 | convolution fusion | flops 67371008 | bytes 2097168 | tf_op jit(solution)/shard_map/ktj,kjf->ktf/dot_general | solution.py:20
  47.5 1.7 copy.10
  49.2 2.1 %fusion.13 = f32[24,128,128]{2,0,1:T(8,128)} fusion(f32[16,128,128]{1,0,2:T(8,128)S(1)} %copy.10, s32[16]{0:T(128)S(1)} %get-tuple-element.35, pred[16]{0:T(512)(128)(4,1)S(1)} %iota_compare_fusion.14), kind=kOutput, calls=%fused_computation.23 | convolution fusion | flops 75498240 | bytes 2621520 | tf_op jit(solution)/shard_map/rk,ktf->rtf/dot_general | solution.py:27
  51.3 1.8 gather_fusion.2
  53.1 2.7 %fusion.27 = f32[16,128,128]{2,1,0:T(8,128)} fusion(bf16[16,128,128]{2,1,0:T(8,128)(2,1)S(1)} %gather_fusion.2, bf16[128,128,128]{2,1,0:T(8,128)(2,1)} %param.10, pred[16]{0:T(512)(128)(4,1)S(1)} %get-tuple-element.44), kind=kOutput, calls=%fused_computation.37 | convolution fusion | flops 67371008 | bytes 2097168 | tf_op jit(solution)/shard_map/ktj,kjf->ktf/dot_general | solution.py:20
  55.8 1.7 copy.11
  57.6 0.0 collective-permute-done.3
  57.6 0.1 collective-permute-start.4
  57.6 2.0 %fusion.11 = f32[24,128,128]{2,0,1:T(8,128)} fusion(f32[16,128,128]{1,0,2:T(8,128)S(1)} %copy.11, s32[16]{0:T(128)S(1)} %get-tuple-element.34, pred[16]{0:T(512)(128)(4,1)S(1)} %iota_compare_fusion.13), kind=kOutput, calls=%fused_computation.21 | convolution fusion | flops 75498240 | bytes 2621520 | tf_op jit(solution)/shard_map/rk,ktf->rtf/dot_general | solution.py:27
  59.7 1.8 gather_fusion.3
  61.5 2.7 %fusion.25 = f32[16,128,128]{2,1,0:T(8,128)} fusion(bf16[16,128,128]{2,1,0:T(8,128)(2,1)S(1)} %gather_fusion.3, bf16[128,128,128]{2,1,0:T(8,128)(2,1)} %param.10, pred[16]{0:T(512)(128)(4,1)S(1)} %get-tuple-element.42), kind=kOutput, calls=%fused_computation.35 | convolution fusion | flops 67371008 | bytes 2097168 | tf_op jit(solution)/shard_map/ktj,kjf->ktf/dot_general | solution.py:20
  64.2 1.7 copy.12
  66.0 2.1 %fusion.9 = f32[24,128,128]{2,0,1:T(8,128)} fusion(f32[16,128,128]{1,0,2:T(8,128)S(1)} %copy.12, s32[16]{0:T(128)S(1)} %get-tuple-element.33, pred[16]{0:T(512)(128)(4,1)S(1)} %iota_compare_fusion.12), kind=kOutput, calls=%fused_computation.19 | convolution fusion | flops 75498240 | bytes 2621520 | tf_op jit(solution)/shard_map/rk,ktf->rtf/dot_general | solution.py:27
  68.0 1.8 gather_fusion.4
  69.8 0.5 collective-permute-done.4
  70.3 0.2 collective-permute-start.5
  70.4 2.7 %fusion.23 = f32[16,128,128]{2,1,0:T(8,128)} fusion(bf16[16,128,128]{2,1,0:T(8,128)(2,1)S(1)} %gather_fusion.4, bf16[128,128,128]{2,1,0:T(8,128)(2,1)} %param.10, pred[16]{0:T(512)(128)(4,1)S(1)} %get-tuple-element.40), kind=kOutput, calls=%fused_computation.33 | convolution fusion | flops 67371008 | bytes 2097168 | tf_op jit(solution)/shard_map/ktj,kjf->ktf/dot_general | solution.py:20
  73.1 1.7 copy.13
  74.9 2.1 %fusion.7 = f32[24,128,128]{2,0,1:T(8,128)} fusion(f32[16,128,128]{1,0,2:T(8,128)S(1)} %copy.13, s32[16]{0:T(128)S(1)} %get-tuple-element.32, pred[16]{0:T(512)(128)(4,1)S(1)} %iota_compare_fusion.11), kind=kOutput, calls=%fused_computation.17 | convolution fusion | flops 75498240 | bytes 2621520 | tf_op jit(solution)/shard_map/rk,ktf->rtf/dot_general | solution.py:27
  77.0 1.8 gather_fusion.5
  78.8 2.7 %fusion.21 = f32[16,128,128]{2,1,0:T(8,128)} fusion(bf16[16,128,128]{2,1,0:T(8,128)(2,1)S(1)} %gather_fusion.5, bf16[128,128,128]{2,1,0:T(8,128)(2,1)} %param.10, pred[16]{0:T(512)(128)(4,1)S(1)} %get-tuple-element.38), kind=kOutput, calls=%fused_computation.31 | convolution fusion | flops 67371008 | bytes 2097168 | tf_op jit(solution)/shard_map/ktj,kjf->ktf/dot_general | solution.py:20
  81.5 1.7 copy.14
  83.2 0.0 collective-permute-done.5
  83.2 3.6 %collective-permute-start.6 = (bf16[3072,128]{1,0:T(8,128)(2,1)}, bf16[3072,128]{1,0:T(8,128)(2,1)}, u32[]{:S(2)}, u32[]{:S(2)}) collective-permute-start(bf16[3072,128]{1,0:T(8,128)(2,1)} %collective-permute-done.5), channel_id=1, source_target_pairs={{0,4},{4,8},{8,12},{12,16},{16,20},{20,24},{24,28},{28,0},{1,5},{5... | collective-permute-start | bytes 2359304 | tf_op jit(solution)/shard_map/ppermute | solution.py:9
  86.8 2.0 %fusion.5 = f32[24,128,128]{2,0,1:T(8,128)} fusion(f32[16,128,128]{1,0,2:T(8,128)S(1)} %copy.14, s32[16]{0:T(128)S(1)} %get-tuple-element.31, pred[16]{0:T(512)(128)(4,1)S(1)} %iota_compare_fusion.10), kind=kOutput, calls=%fused_computation.15 | convolution fusion | flops 75498240 | bytes 2621520 | tf_op jit(solution)/shard_map/rk,ktf->rtf/dot_general | solution.py:27
  88.9 1.8 gather_fusion.6
  90.7 2.8 %fusion.19 = f32[16,128,128]{2,1,0:T(8,128)} fusion(bf16[16,128,128]{2,1,0:T(8,128)(2,1)S(1)} %gather_fusion.6, bf16[128,128,128]{2,1,0:T(8,128)(2,1)} %param.10, pred[16]{0:T(512)(128)(4,1)S(1)} %get-tuple-element.50), kind=kOutput, calls=%fused_computation.29 | convolution fusion | flops 67371008 | bytes 2097168 | tf_op jit(solution)/shard_map/ktj,kjf->ktf/dot_general | solution.py:20
  93.4 1.7 copy.15
  95.2 2.1 %fusion.3 = f32[24,128,128]{2,0,1:T(8,128)} fusion(f32[16,128,128]{1,0,2:T(8,128)S(1)} %copy.15, s32[16]{0:T(128)S(1)} %get-tuple-element.37, pred[16]{0:T(512)(128)(4,1)S(1)} %iota_compare_fusion.9), kind=kOutput, calls=%fused_computation.13 | convolution fusion | flops 75498240 | bytes 2621520 | tf_op jit(solution)/shard_map/rk,ktf->rtf/dot_general | solution.py:27
  97.3 0.0 collective-permute-done.6
  97.3 1.8 gather_fusion.7
  99.1 2.7 %fusion.17 = f32[16,128,128]{2,1,0:T(8,128)} fusion(bf16[16,128,128]{2,1,0:T(8,128)(2,1)S(1)} %gather_fusion.7, bf16[128,128,128]{2,1,0:T(8,128)(2,1)} %param.10, pred[16]{0:T(512)(128)(4,1)S(1)} %get-tuple-element.6), kind=kOutput, calls=%fused_computation.27 | convolution fusion | flops 67371008 | bytes 2097168 | tf_op jit(solution)/shard_map/ktj,kjf->ktf/dot_general | solution.py:20
  101.8 1.7 copy.16
  103.5 5.0 %add_convert_fusion = bf16[24,128,128]{2,0,1:T(8,128)(2,1)S(1)} fusion(f32[24,128,128]{2,0,1:T(8,128)} %fusion.3, f32[24,128,128]{2,0,1:T(8,128)} %fusion.5, f32[24,128,128]{2,0,1:T(8,128)} %fusion.7, f32[24,128,128]{2,0,1:T(8,128)} %fusion.9, f32[24,128,128]{2,0,1:T(8,128)} %fusion.11, f32[24,128,128]{2,0,1:T(8,128)S(1)} %fusion.15, ...), kind=kOutput, calls=%fused_computation.11 | convolution fusion | flops 78643968 | bytes 12845136 | tf_op jit(solution)/shard_map/rk,ktf->rtf/dot_general | solution.py:27
  108.6 0.0 copy-start.3
  108.6 1.1 copy.8
  109.6 0.0 all-gather.2.cloned.1.call-update
  109.7 63.5 %all-gather.2.cloned.1.call-done = bf16[3072,512]{1,0:T(8,128)(2,1)} async-done(((bf16[3072,128]{1,0:T(8,128)(2,1)}), bf16[3072,512]{1,0:T(8,128)(2,1)}) %all-gather.2.cloned.1.call-update) | async-done | bytes 3145744 | tf_op jit(solution)/shard_map/all_gather | solution.py:52
  173.2 3.8 %fusion.1 = bf16[3072,128]{1,0:T(8,128)(2,1)} fusion(bf16[3072,512]{1,0:T(8,128)(2,1)} %all-gather.2.cloned.1.call-done, f32[128]{0:T(128)S(1)} %copy-done.3, bf16[512,512]{1,0:T(8,128)(2,1)S(1)} %copy-done, s32[]{:T(128)S(6)} %select_n.10), kind=kOutput, calls=%fused_computation.10 | convolution fusion | flops 403832832 | bytes 4063748 | tf_op jit(solution)/shard_map/dot_general | solution.py:51
  (14 shorter events, 0.1 us)
Async XLA Ops:
  6.5 166.7 %copy-start = (bf16[512,512]{1,0:T(8,128)(2,1)S(1)}, bf16[512,512]{1,0:T(8,128)(2,1)}, u32[]{:S(2)}) copy-start(bf16[512,512]{1,0:T(8,128)(2,1)} %param.14) | copy-start | bytes 1572868
  6.5 166.7 %all-gather.2.cloned.1.call-start = ((), (), s32[]{:S(2)}) async-start(), calls=%async_computation | async-start | bytes 3932160 | tf_op jit(solution)/shard_map/all_gather | solution.py:52
  6.5 13.2 %collective-permute-start = (bf16[3072,128]{1,0:T(8,128)(2,1)}, bf16[3072,128]{1,0:T(8,128)(2,1)S(1)}, u32[]{:S(2)}, u32[]{:S(2)}) collective-permute-start(bf16[3072,128]{1,0:T(8,128)(2,1)} %param.9), channel_id=1, source_target_pairs={{0,4},{4,8},{8,12},{12,16},{16,20},{20,24},{24,28},{28,0},{1,5},{5... | collective-permute-start | bytes 2359304 | tf_op jit(solution)/shard_map/ppermute | solution.py:9
  19.8 12.4 %copy-start.1 = (bf16[3072,128]{1,0:T(8,128)(2,1)}, bf16[3072,128]{1,0:T(8,128)(2,1)S(1)}, u32[]{:S(2)}) copy-start(bf16[3072,128]{1,0:T(8,128)(2,1)S(1)} %collective-permute-done) | copy-start | bytes 2359300
  19.8 12.4 %collective-permute-start.1 = (bf16[3072,128]{1,0:T(8,128)(2,1)S(1)}, bf16[3072,128]{1,0:T(8,128)(2,1)}, u32[]{:S(2)}, u32[]{:S(2)}) collective-permute-start(bf16[3072,128]{1,0:T(8,128)(2,1)S(1)} %collective-permute-done), channel_id=1, source_target_pairs={{0,4},{4,8},{8,12},{12,16},{16,20},{20,24},{24,28},{28,0},{1,5},{5... | collective-permute-start | bytes 2359304 | tf_op jit(solution)/shard_map/ppermute | solution.py:9
  22.1 11.3 %copy-start.2 = (s32[128]{0:T(128)S(1)}, s32[128]{0:T(128)}, u32[]{:S(2)}) copy-start(s32[128]{0:T(128)} %param.11) | copy-start | bytes 1540
  32.2 12.6 %collective-permute-start.2 = (bf16[3072,128]{1,0:T(8,128)(2,1)}, bf16[3072,128]{1,0:T(8,128)(2,1)}, u32[]{:S(2)}, u32[]{:S(2)}) collective-permute-start(bf16[3072,128]{1,0:T(8,128)(2,1)} %collective-permute-done.1), channel_id=1, source_target_pairs={{0,4},{4,8},{8,12},{12,16},{16,20},{20,24},{24,28},{28,0},{1,5},{5... | collective-permute-start | bytes 2359304 | tf_op jit(solution)/shard_map/ppermute | solution.py:9
  44.8 12.8 %collective-permute-start.3 = (bf16[3072,128]{1,0:T(8,128)(2,1)}, bf16[3072,128]{1,0:T(8,128)(2,1)}, u32[]{:S(2)}, u32[]{:S(2)}) collective-permute-start(bf16[3072,128]{1,0:T(8,128)(2,1)} %collective-permute-done.2), channel_id=1, source_target_pairs={{0,4},{4,8},{8,12},{12,16},{16,20},{20,24},{24,28},{28,0},{1,5},{5... | collective-permute-start | bytes 2359304 | tf_op jit(solution)/shard_map/ppermute | solution.py:9
  57.6 12.7 %collective-permute-start.4 = (bf16[3072,128]{1,0:T(8,128)(2,1)}, bf16[3072,128]{1,0:T(8,128)(2,1)}, u32[]{:S(2)}, u32[]{:S(2)}) collective-permute-start(bf16[3072,128]{1,0:T(8,128)(2,1)} %collective-permute-done.3), channel_id=1, source_target_pairs={{0,4},{4,8},{8,12},{12,16},{16,20},{20,24},{24,28},{28,0},{1,5},{5... | collective-permute-start | bytes 2359304 | tf_op jit(solution)/shard_map/ppermute | solution.py:9
  70.3 13.0 %collective-permute-start.5 = (bf16[3072,128]{1,0:T(8,128)(2,1)}, bf16[3072,128]{1,0:T(8,128)(2,1)}, u32[]{:S(2)}, u32[]{:S(2)}) collective-permute-start(bf16[3072,128]{1,0:T(8,128)(2,1)} %collective-permute-done.4), channel_id=1, source_target_pairs={{0,4},{4,8},{8,12},{12,16},{16,20},{20,24},{24,28},{28,0},{1,5},{5... | collective-permute-start | bytes 2359304 | tf_op jit(solution)/shard_map/ppermute | solution.py:9
  83.2 14.1 %collective-permute-start.6 = (bf16[3072,128]{1,0:T(8,128)(2,1)}, bf16[3072,128]{1,0:T(8,128)(2,1)}, u32[]{:S(2)}, u32[]{:S(2)}) collective-permute-start(bf16[3072,128]{1,0:T(8,128)(2,1)} %collective-permute-done.5), channel_id=1, source_target_pairs={{0,4},{4,8},{8,12},{12,16},{16,20},{20,24},{24,28},{28,0},{1,5},{5... | collective-permute-start | bytes 2359304 | tf_op jit(solution)/shard_map/ppermute | solution.py:9
  108.6 64.7 %copy-start.3 = (f32[128]{0:T(128)S(1)}, f32[128]{0:T(128)}, u32[]{:S(2)}) copy-start(f32[128]{0:T(128)} %param.15) | copy-start | bytes 1540
Sparse Core Ops, SparseCore 0:
  109.8 63.3 all-gather.1
where the time goes:
time: 185 us; the launch traced here: 184 us
  waiting for transfers between devices  87.2 us (47%)
  matrix products  42.9 us (23%)
  local copies, waits for them, and re-layouts  29.6 us (16%)
  between operations  13.7 us (7%)
  other arithmetic  6.13 us (3%)
  starting transfers between devices  4.29 us (2%)
    all_gather x1, waiting for transfers between devices, body(): lax.all_gather(aggregate, 'feat', axis=1, tiled=True)  63.5 us
    ppermute x7, waiting for transfers between devices, shifted(): lax.ppermute(shard, axis, [(i, (i + by) % count) for i in range(count)])  23.6 us
    dot_general x8, matrix products, add_tiles(): jnp.einsum('ktj,kjf->ktf', values_all[offset], picked, preferred_element_...  20.8 us
    dot_general x8, matrix products, add_tiles(): jnp.einsum('rk,ktf->rtf', one_hot, products, precision=lax.Precision.HIGH...  18.4 us
    gather x8, local copies, waits for them, and re-layouts, pick_tiles(): return jnp.take(source, wanted, axis=0)  14.2 us
    dot_general x8, local copies, waits for them, and re-layouts, add_tiles(): jnp.einsum('ktj,kjf->ktf', values_all[offset], picked, preferred_element_...  12.6 us
    lt x8, other arithmetic, add_tiles(): active = jnp.arange(slot_count) < tile_counts[offset]  5.05 us
    ppermute x7, starting transfers between devices, shifted(): lax.ppermute(shard, axis, [(i, (i + by) % count) for i in range(count)])  4.28 us
  transfers between devices with their start and end apart: 8, of which 5 were waited for; matrix products, arithmetic and copies ran while one was open for 34% of the time, Pallas kernels for 0%

commit v1 on v0

--- a/solution.py
+++ b/solution.py
@@ -2,6 +2,27 @@
 import jax.numpy as jnp
 from jax import lax
 from jax.sharding import PartitionSpec as P
+
+
+def joined_along(blocks, dim):
+    shape = list(blocks.shape[1:])
+    shape[dim] *= blocks.shape[0]
+    return jnp.moveaxis(blocks, 0, dim).reshape(shape)
+
+
+def collected_by_bits(x, axis):
+    size, index = (lax.axis_size(axis), lax.axis_index(axis))
+    parts, bit = (x[None], 1)
+    while bit < size:
+        theirs = lax.ppermute(parts, axis, [(i, i ^ bit) for i in range(size)])
+        low = index & bit == 0
+        parts = jnp.concatenate([jnp.where(low, parts, theirs), jnp.where(low, theirs, parts)])
+        bit *= 2
+    return parts
+
+
+def gather_by_bits(array, axis, dim):
+    return joined_along(collected_by_bits(array, axis), dim)
 
 
 def shifted(shard, axis, by):
@@ -49,9 +70,7 @@
     member = lax.axis_index("feat")
     own_cols = lax.dynamic_slice_in_dim(weight, member * out_width, out_width, 1)
     mixed = jnp.dot(
-        lax.all_gather(aggregate, "feat", axis=1, tiled=True),
-        own_cols,
-        preferred_element_type=jnp.float32,
+        gather_by_bits(aggregate, "feat", 1), own_cols, preferred_element_type=jnp.float32
     )
     return jnp.maximum(mixed + bias[None, :], 0.0).astype(jnp.bfloat16)
 

time: 185 us -> 209 us (1.13)
  waiting for transfers between devices: 87.2 us -> 109 us
  between operations: 13.7 us -> 0.33 us
  other arithmetic: 6.13 us -> 12.3 us
  local copies, waits for them, and re-layouts: 29.6 us -> 34.3 us
  starting transfers between devices: 4.29 us -> 8.51 us
    ppermute x0 -> x2, waiting for transfers between devices: none -> 85.7 us  [collected_by_bits(): theirs = lax.ppermute(parts, axis, [(i, i ^ bit) for i in range(size)])]
    all_gather x1 -> x0, waiting for transfers between devices: 63.5 us -> none  [body(): lax.all_gather(aggregate, 'feat', axis=1, tiled=True)]
    transpose x0 -> x1, local copies, waits for them, and re-layouts: none -> 4.68 us  [joined_along(): return jnp.moveaxis(blocks, 0, dim).reshape(shape)]
    ppermute x0 -> x2, starting transfers between devices: none -> 4.23 us  [collected_by_bits(): theirs = lax.ppermute(parts, axis, [(i, i ^ bit) for i in range(size)])]
    select_n x0 -> x2, other arithmetic: none -> 2.85 us  [collected_by_bits(): jnp.where(low, parts, theirs)]
  transfers between devices with their start and end apart: 8 -> 9, of which waited for: 5 -> 6; matrix products, arithmetic and copies ran while one was open for 34% -> 30% of each run, Pallas kernels for 0% -> 0%
where the time goes in v1:
time: 209 us; the launch traced here: 208 us
  waiting for transfers between devices  109 us (52%)
  matrix products  43 us (21%)
  local copies, waits for them, and re-layouts  34.3 us (16%)
  other arithmetic  12.3 us (6%)
  starting transfers between devices  8.51 us (4%)
    ppermute x2, waiting for transfers between devices, collected_by_bits(): theirs = lax.ppermute(parts, axis, [(i, i ^ bit) for i in range(size)])  85.7 us
    ppermute x7, waiting for transfers between devices, shifted(): lax.ppermute(shard, axis, [(i, (i + by) % count) for i in range(count)])  23.5 us
    dot_general x8, matrix products, add_tiles(): jnp.einsum('ktj,kjf->ktf', values_all[offset], picked, preferred_element_...  20.8 us
    dot_general x8, matrix products, add_tiles(): jnp.einsum('rk,ktf->rtf', one_hot, products, precision=lax.Precision.HIGH...  18.4 us
    gather x8, local copies, waits for them, and re-layouts, pick_tiles(): return jnp.take(source, wanted, axis=0)  14.2 us
    dot_general x8, local copies, waits for them, and re-layouts, add_tiles(): jnp.einsum('ktj,kjf->ktf', values_all[offset], picked, preferred_element_...  12.6 us
    lt x8, other arithmetic, add_tiles(): active = jnp.arange(slot_count) < tile_counts[offset]  5.12 us
    transpose x1, local copies, waits for them, and re-layouts, joined_along(): return jnp.moveaxis(blocks, 0, dim).reshape(shape)  4.68 us
  transfers between devices with their start and end apart: 9, of which 6 were waited for; matrix products, arithmetic and copies ran while one was open for 30% of the time, Pallas kernels for 0%

profile of v1, /device:TPU:0, one launch (start us, length us, event | category | flops | bytes accessed | tf_op | source)
XLA Modules:
  0.0 207.6 jit_solution(6114836454986154973)
XLA Ops:
  0.0 0.5 collective-permute-start
  0.5 1.0 compare_and_fusion
  1.5 1.6 fusion.107
  3.1 1.8 gather_fusion
  4.9 0.6 iota_compare_fusion.9
  5.6 0.7 iota_compare_fusion.10
  6.2 0.6 iota_compare_fusion.11
  6.8 0.6 iota_compare_fusion.12
  7.4 0.6 iota_compare_fusion.13
  8.1 0.6 iota_compare_fusion.14
  8.7 4.5 %collective-permute-done = bf16[3072,128]{1,0:T(8,128)(2,1)S(1)} collective-permute-done((bf16[3072,128]{1,0:T(8,128)(2,1)}, bf16[3072,128]{1,0:T(8,128)(2,1)S(1)}, u32[]{:S(2)}, u32[]{:S(2)}) %collective-permute-start) | collective-permute-done | bytes 786464 | tf_op jit(solution)/shard_map/ppermute | solution.py:30
  13.2 0.0 collective-permute-start.1
  13.2 0.7 iota_compare_fusion.15
  14.0 1.7 fusion.31
  15.7 9.9 %collective-permute-done.1 = bf16[3072,128]{1,0:T(8,128)(2,1)} collective-permute-done((bf16[3072,128]{1,0:T(8,128)(2,1)S(1)}, bf16[3072,128]{1,0:T(8,128)(2,1)}, u32[]{:S(2)}, u32[]{:S(2)}) %collective-permute-start.1) | collective-permute-done | bytes 786464 | tf_op jit(solution)/shard_map/ppermute | solution.py:30
  25.6 0.7 iota_compare_fusion.8
  26.3 0.5 copy.10
  26.9 0.1 fusion.108
  27.0 0.9 fusion.15
  27.9 1.8 gather_fusion.1
  29.7 8.6 %collective-permute-done.2 = bf16[3072,128]{1,0:T(8,128)(2,1)} collective-permute-done((bf16[3072,128]{1,0:T(8,128)(2,1)}, bf16[3072,128]{1,0:T(8,128)(2,1)}, u32[]{:S(2)}, u32[]{:S(2)}) %collective-permute-start.2) | collective-permute-done | bytes 786464 | tf_op jit(solution)/shard_map/ppermute | solution.py:30
  38.3 2.7 %fusion.29 = f32[16,128,128]{2,1,0:T(8,128)} fusion(bf16[16,128,128]{2,1,0:T(8,128)(2,1)S(1)} %gather_fusion.1, bf16[128,128,128]{2,1,0:T(8,128)(2,1)} %param.10, pred[16]{0:T(512)(128)(4,1)S(1)} %get-tuple-element.50), kind=kOutput, calls=%fused_computation.45 | convolution fusion | flops 67371008 | bytes 2097168 | tf_op jit(solution)/shard_map/ktj,kjf->ktf/dot_general | solution.py:41
  41.0 1.7 copy.11
  42.7 2.1 fusion.13
  44.8 1.8 gather_fusion.2
  46.6 2.7 %fusion.27 = f32[16,128,128]{2,1,0:T(8,128)} fusion(bf16[16,128,128]{2,1,0:T(8,128)(2,1)S(1)} %gather_fusion.2, bf16[128,128,128]{2,1,0:T(8,128)(2,1)} %param.10, pred[16]{0:T(512)(128)(4,1)S(1)} %get-tuple-element.48), kind=kOutput, calls=%fused_computation.43 | convolution fusion | flops 67371008 | bytes 2097168 | tf_op jit(solution)/shard_map/ktj,kjf->ktf/dot_general | solution.py:41
  49.3 1.7 copy.12
  51.0 0.1 collective-permute-start.4
  51.1 2.0 fusion.11
  53.1 1.8 gather_fusion.3
  54.9 2.7 %fusion.25 = f32[16,128,128]{2,1,0:T(8,128)} fusion(bf16[16,128,128]{2,1,0:T(8,128)(2,1)S(1)} %gather_fusion.3, bf16[128,128,128]{2,1,0:T(8,128)(2,1)} %param.10, pred[16]{0:T(512)(128)(4,1)S(1)} %get-tuple-element.46), kind=kOutput, calls=%fused_computation.41 | convolution fusion | flops 67371008 | bytes 2097168 | tf_op jit(solution)/shard_map/ktj,kjf->ktf/dot_general | solution.py:41
  57.6 1.7 copy.13
  59.4 2.1 fusion.9
  61.4 1.8 gather_fusion.4
  63.2 0.5 collective-permute-done.4
  63.7 0.1 collective-permute-start.5
  63.9 2.7 %fusion.23 = f32[16,128,128]{2,1,0:T(8,128)} fusion(bf16[16,128,128]{2,1,0:T(8,128)(2,1)S(1)} %gather_fusion.4, bf16[128,128,128]{2,1,0:T(8,128)(2,1)} %param.10, pred[16]{0:T(512)(128)(4,1)S(1)} %get-tuple-element.44), kind=kOutput, calls=%fused_computation.39 | convolution fusion | flops 67371008 | bytes 2097168 | tf_op jit(solution)/shard_map/ktj,kjf->ktf/dot_general | solution.py:41
  66.6 1.7 copy.14
  68.3 2.1 %fusion.7 = f32[24,128,128]{2,0,1:T(8,128)} fusion(f32[16,128,128]{1,0,2:T(8,128)S(1)} %copy.14, s32[16]{0:T(128)S(1)} %get-tuple-element.36, pred[16]{0:T(512)(128)(4,1)S(1)} %iota_compare_fusion.11), kind=kOutput, calls=%fused_computation.21 | convolution fusion | flops 75498240 | bytes 2621520 | tf_op jit(solution)/shard_map/rk,ktf->rtf/dot_general | solution.py:48
  70.4 1.8 gather_fusion.5
  72.2 2.7 %fusion.21 = f32[16,128,128]{2,1,0:T(8,128)} fusion(bf16[16,128,128]{2,1,0:T(8,128)(2,1)S(1)} %gather_fusion.5, bf16[128,128,128]{2,1,0:T(8,128)(2,1)} %param.10, pred[16]{0:T(512)(128)(4,1)S(1)} %get-tuple-element.42), kind=kOutput, calls=%fused_computation.37 | convolution fusion | flops 67371008 | bytes 2097168 | tf_op jit(solution)/shard_map/ktj,kjf->ktf/dot_general | solution.py:41
  74.9 1.7 copy.15
  76.7 3.6 %collective-permute-start.6 = (bf16[3072,128]{1,0:T(8,128)(2,1)}, bf16[3072,128]{1,0:T(8,128)(2,1)}, u32[]{:S(2)}, u32[]{:S(2)}) collective-permute-start(bf16[3072,128]{1,0:T(8,128)(2,1)} %collective-permute-done.5), channel_id=1, source_target_pairs={{0,4},{4,8},{8,12},{12,16},{16,20},{20,24},{24,28},{28,0},{1,5},{5... | collective-permute-start | bytes 2359304 | tf_op jit(solution)/shard_map/ppermute | solution.py:30
  80.3 2.1 fusion.5
  82.3 1.8 gather_fusion.6
  84.1 2.8 %fusion.19 = f32[16,128,128]{2,1,0:T(8,128)} fusion(bf16[16,128,128]{2,1,0:T(8,128)(2,1)S(1)} %gather_fusion.6, bf16[128,128,128]{2,1,0:T(8,128)(2,1)} %param.10, pred[16]{0:T(512)(128)(4,1)S(1)} %get-tuple-element.54), kind=kOutput, calls=%fused_computation.35 | convolution fusion | flops 67371008 | bytes 2097168 | tf_op jit(solution)/shard_map/ktj,kjf->ktf/dot_general | solution.py:41
  86.9 1.7 copy.16
  88.6 2.1 %fusion.3 = f32[24,128,128]{2,0,1:T(8,128)} fusion(f32[16,128,128]{1,0,2:T(8,128)S(1)} %copy.16, s32[16]{0:T(128)S(1)} %get-tuple-element.41, pred[16]{0:T(512)(128)(4,1)S(1)} %iota_compare_fusion.9), kind=kOutput, calls=%fused_computation.17 | convolution fusion | flops 75498240 | bytes 2621520 | tf_op jit(solution)/shard_map/rk,ktf->rtf/dot_general | solution.py:48
  90.7 1.8 gather_fusion.7
  92.5 2.7 %fusion.17 = f32[16,128,128]{2,1,0:T(8,128)} fusion(bf16[16,128,128]{2,1,0:T(8,128)(2,1)S(1)} %gather_fusion.7, bf16[128,128,128]{2,1,0:T(8,128)(2,1)} %param.10, pred[16]{0:T(512)(128)(4,1)S(1)} %get-tuple-element.6), kind=kOutput, calls=%fused_computation.33 | convolution fusion | flops 67371008 | bytes 2097168 | tf_op jit(solution)/shard_map/ktj,kjf->ktf/dot_general | solution.py:41
  95.2 1.7 copy.17
  97.0 5.0 %add_convert_fusion = bf16[24,128,128]{2,0,1:T(8,128)(2,1)S(1)} fusion(f32[24,128,128]{2,0,1:T(8,128)} %fusion.3, f32[24,128,128]{2,0,1:T(8,128)} %fusion.5, f32[24,128,128]{2,0,1:T(8,128)} %fusion.7, f32[24,128,128]{2,0,1:T(8,128)} %fusion.9, f32[24,128,128]{2,0,1:T(8,128)} %fusion.11, f32[24,128,128]{2,0,1:T(8,128)S(1)} %fusion.15, ...), kind=kOutput, calls=%fused_computation.13 | convolution fusion | flops 78643968 | bytes 12845136 | tf_op jit(solution)/shard_map/rk,ktf->rtf/dot_general | solution.py:48
  102.0 0.2 copy.8
  102.2 1.6 collective-permute-start.7
  103.8 17.9 %collective-permute-done.7 = bf16[1,3072,128]{2,1,0:T(8,128)(2,1)S(1)} collective-permute-done((bf16[1,3072,128]{2,1,0:T(8,128)(2,1)S(1)}, bf16[1,3072,128]{2,1,0:T(8,128)(2,1)S(1)}, u32[]{:S(2)}, u32[]{:S(2)}) %collective-permute-start.7) | collective-permute-done | bytes 786464 | tf_op jit(solution)/shard_map/ppermute | solution.py:17
  121.7 0.9 copy-done.1
  122.6 1.2 broadcast_select_fusion.3
  123.8 1.3 pad_maximum_fusion
  125.1 2.6 %collective-permute-start.8 = (bf16[2,3072,128]{2,1,0:T(8,128)(2,1)}, bf16[2,3072,128]{2,1,0:T(8,128)(2,1)}, u32[]{:S(2)}, u32[]{:S(2)}) collective-permute-start(bf16[2,3072,128]{2,1,0:T(8,128)(2,1)} %pad_maximum_fusion), channel_id=1, source_target_pairs={{0,2},{1,3},{2,0},{3,1},{4,6},{5,7},{6,4},{7,5},{8,10},{9,11},{10,... | collective-permute-start | bytes 4718600 | tf_op jit(solution)/shard_map/ppermute | solution.py:17
  127.7 67.8 %collective-permute-done.8 = bf16[2,3072,128]{2,1,0:T(8,128)(2,1)} collective-permute-done((bf16[2,3072,128]{2,1,0:T(8,128)(2,1)}, bf16[2,3072,128]{2,1,0:T(8,128)(2,1)}, u32[]{:S(2)}, u32[]{:S(2)}) %collective-permute-start.8) | collective-permute-done | bytes 1572896 | tf_op jit(solution)/shard_map/ppermute | solution.py:17
  195.5 1.6 broadcast_select_fusion.1
  197.2 1.9 maximum_bitcast_fusion
  199.1 4.7 %copy.9 = bf16[3072,4,128]{0,2,1:T(8,128)(2,1)} copy(bf16[3072,4,128]{2,0,1:T(8,128)(2,1)} %maximum_bitcast_fusion) | data formatting | bytes 6291456 | tf_op jit(solution)/shard_map/transpose | solution.py:10
  203.8 3.8 %fusion.1 = bf16[3072,128]{1,0:T(8,128)(2,1)} fusion(bf16[3072,512]{0,1:T(8,128)(2,1)} %bitcast.72, f32[128]{0:T(128)S(1)} %copy-done.4, bf16[512,512]{1,0:T(8,128)(2,1)S(1)} %copy-done, s32[]{:T(128)S(6)} %select_n.40), kind=kOutput, calls=%fused_computation.10 | convolution fusion | flops 403832832 | bytes 4063748 | tf_op jit(solution)/shard_map/dot_general | solution.py:72
  (22 shorter events, 0.1 us)
Async XLA Ops:
  0.0 203.8 %copy-start = (bf16[512,512]{1,0:T(8,128)(2,1)S(1)}, bf16[512,512]{1,0:T(8,128)(2,1)}, u32[]{:S(2)}) copy-start(bf16[512,512]{1,0:T(8,128)(2,1)} %param.14) | copy-start | bytes 1572868
  0.0 13.2 %collective-permute-start = (bf16[3072,128]{1,0:T(8,128)(2,1)}, bf16[3072,128]{1,0:T(8,128)(2,1)S(1)}, u32[]{:S(2)}, u32[]{:S(2)}) collective-permute-start(bf16[3072,128]{1,0:T(8,128)(2,1)} %param.9), channel_id=1, source_target_pairs={{0,4},{4,8},{8,12},{12,16},{16,20},{20,24},{24,28},{28,0},{1,5},{5... | collective-permute-start | bytes 2359304 | tf_op jit(solution)/shard_map/ppermute | solution.py:30
  13.2 12.4 %copy-start.2 = (bf16[3072,128]{1,0:T(8,128)(2,1)}, bf16[3072,128]{1,0:T(8,128)(2,1)S(1)}, u32[]{:S(2)}) copy-start(bf16[3072,128]{1,0:T(8,128)(2,1)S(1)} %collective-permute-done) | copy-start | bytes 2359300
  13.2 12.4 %collective-permute-start.1 = (bf16[3072,128]{1,0:T(8,128)(2,1)S(1)}, bf16[3072,128]{1,0:T(8,128)(2,1)}, u32[]{:S(2)}, u32[]{:S(2)}) collective-permute-start(bf16[3072,128]{1,0:T(8,128)(2,1)S(1)} %collective-permute-done), channel_id=1, source_target_pairs={{0,4},{4,8},{8,12},{12,16},{16,20},{20,24},{24,28},{28,0},{1,5},{5... | collective-permute-start | bytes 2359304 | tf_op jit(solution)/shard_map/ppermute | solution.py:30
  15.7 11.2 %copy-start.3 = (s32[128]{0:T(128)S(1)}, s32[128]{0:T(128)}, u32[]{:S(2)}) copy-start(s32[128]{0:T(128)} %param.11) | copy-start | bytes 1540
  25.6 12.6 %collective-permute-start.2 = (bf16[3072,128]{1,0:T(8,128)(2,1)}, bf16[3072,128]{1,0:T(8,128)(2,1)}, u32[]{:S(2)}, u32[]{:S(2)}) collective-permute-start(bf16[3072,128]{1,0:T(8,128)(2,1)} %collective-permute-done.1), channel_id=1, source_target_pairs={{0,4},{4,8},{8,12},{12,16},{16,20},{20,24},{24,28},{28,0},{1,5},{5... | collective-permute-start | bytes 2359304 | tf_op jit(solution)/shard_map/ppermute | solution.py:30
  38.3 12.8 %collective-permute-start.3 = (bf16[3072,128]{1,0:T(8,128)(2,1)}, bf16[3072,128]{1,0:T(8,128)(2,1)}, u32[]{:S(2)}, u32[]{:S(2)}) collective-permute-start(bf16[3072,128]{1,0:T(8,128)(2,1)} %collective-permute-done.2), channel_id=1, source_target_pairs={{0,4},{4,8},{8,12},{12,16},{16,20},{20,24},{24,28},{28,0},{1,5},{5... | collective-permute-start | bytes 2359304 | tf_op jit(solution)/shard_map/ppermute | solution.py:30
  51.0 12.7 %collective-permute-start.4 = (bf16[3072,128]{1,0:T(8,128)(2,1)}, bf16[3072,128]{1,0:T(8,128)(2,1)}, u32[]{:S(2)}, u32[]{:S(2)}) collective-permute-start(bf16[3072,128]{1,0:T(8,128)(2,1)} %collective-permute-done.3), channel_id=1, source_target_pairs={{0,4},{4,8},{8,12},{12,16},{16,20},{20,24},{24,28},{28,0},{1,5},{5... | collective-permute-start | bytes 2359304 | tf_op jit(solution)/shard_map/ppermute | solution.py:30
  63.7 12.9 %collective-permute-start.5 = (bf16[3072,128]{1,0:T(8,128)(2,1)}, bf16[3072,128]{1,0:T(8,128)(2,1)}, u32[]{:S(2)}, u32[]{:S(2)}) collective-permute-start(bf16[3072,128]{1,0:T(8,128)(2,1)} %collective-permute-done.4), channel_id=1, source_target_pairs={{0,4},{4,8},{8,12},{12,16},{16,20},{20,24},{24,28},{28,0},{1,5},{5... | collective-permute-start | bytes 2359304 | tf_op jit(solution)/shard_map/ppermute | solution.py:30
  76.7 14.1 %collective-permute-start.6 = (bf16[3072,128]{1,0:T(8,128)(2,1)}, bf16[3072,128]{1,0:T(8,128)(2,1)}, u32[]{:S(2)}, u32[]{:S(2)}) collective-permute-start(bf16[3072,128]{1,0:T(8,128)(2,1)} %collective-permute-done.5), channel_id=1, source_target_pairs={{0,4},{4,8},{8,12},{12,16},{16,20},{20,24},{24,28},{28,0},{1,5},{5... | collective-permute-start | bytes 2359304 | tf_op jit(solution)/shard_map/ppermute | solution.py:30
  102.2 19.5 %collective-permute-start.7 = (bf16[1,3072,128]{2,1,0:T(8,128)(2,1)S(1)}, bf16[1,3072,128]{2,1,0:T(8,128)(2,1)S(1)}, u32[]{:S(2)}, u32[]{:S(2)}) collective-permute-start(bf16[1,3072,128]{2,1,0:T(8,128)(2,1)S(1)} %bitcast.73), channel_id=1, source_target_pairs={{0,1},{1,0},{2,3},{3,2},{4,5},{5,4},{6,7},{7,6},{8,9},{9,8},{10,11... | collective-permute-start | bytes 2359304 | tf_op jit(solution)/shard_map/ppermute | solution.py:17
  121.7 0.9 copy-start.1
  125.1 70.4 %collective-permute-start.8 = (bf16[2,3072,128]{2,1,0:T(8,128)(2,1)}, bf16[2,3072,128]{2,1,0:T(8,128)(2,1)}, u32[]{:S(2)}, u32[]{:S(2)}) collective-permute-start(bf16[2,3072,128]{2,1,0:T(8,128)(2,1)} %pad_maximum_fusion), channel_id=1, source_target_pairs={{0,2},{1,3},{2,0},{3,1},{4,6},{5,7},{6,4},{7,5},{8,10},{9,11},{10,... | collective-permute-start | bytes 4718600 | tf_op jit(solution)/shard_map/ppermute | solution.py:17
  199.1 4.7 %copy-start.4 = (f32[128]{0:T(128)S(1)}, f32[128]{0:T(128)}, u32[]{:S(2)}) copy-start(f32[128]{0:T(128)} %param.15) | copy-start | bytes 1540
